TPU v7x, 32 devices: a whole 2x2x4 slice. The times are simulated.
32 devices in a mesh: dp: 8 (over y, x, core), tensor: 4 (over z).
Axes of the slice: x: 2, y: 2, z: 4, core: 2. Of those that a mesh axis runs over, the one named last changes fastest.
Arguments:
- short_tokens: bfloat16 [16, 256, 768], P('dp'), may hold values from -6 to 6
- short_lengths: int32 [16], P('dp'), may hold values from 64 to 256, as said below
- long_tokens: bfloat16 [24, 512, 768], P('dp'), may hold values from -6 to 6
- long_lengths: int32 [24], P('dp'), may hold values from 257 to 512, as said below
- w_qkv: bfloat16 [3, 768, 768], P(None, None, 'tensor'), may hold values from -0.21875 to 0.21875
- b_qv: bfloat16 [2, 12, 64], P(None, 'tensor'), may hold values from -3 to 3
- w_out: bfloat16 [768, 768], P('tensor'), may hold values from -2.5 to 2.5
- res_biases: bfloat16 [2, 768], replicated, may hold values from -3 to 3
- ln_gains: bfloat16 [2, 768], replicated, may hold values from 0.099609375 to 1.8984375
- ln_shifts: bfloat16 [2, 768], replicated, may hold values from -3 to 3
- w_up: bfloat16 [768, 3072], P(None, 'tensor'), may hold values from -0.21875 to 0.21875
- b_up: bfloat16 [4, 768], P('tensor'), may hold values from -3 to 3
- w_down: bfloat16 [3072, 768], P('tensor'), may hold values from -0.109375 to 0.109375
- short_cotangent: bfloat16 [16, 256, 768], P('dp'), may hold values from -6 to 6
- long_cotangent: bfloat16 [24, 512, 768], P('dp'), may hold values from -6 to 6
Outputs:
- short_encoded: bfloat16 [16, 256, 768], P('dp')
- long_encoded: bfloat16 [24, 512, 768], P('dp')
- short_grad_tokens: float32 [16, 256, 768], P('dp')
- long_grad_tokens: float32 [24, 512, 768], P('dp')
- grad_qkv: float32 [3, 768, 768], P(None, 'dp', 'tensor')
- grad_qv_bias: float32 [2, 12, 64], P(None, 'tensor', 'dp')
- grad_out: float32 [768, 768], P('tensor', 'dp')
- grad_res_biases: float32 [2, 768], P(None, 'dp')
- grad_gains: float32 [2, 768], P(None, 'dp')
- grad_shifts: float32 [2, 768], P(None, 'dp')
- grad_up: float32 [768, 3072], P('dp', 'tensor')
- grad_up_bias: float32 [4, 768], P('tensor', 'dp')
- grad_down: float32 [3072, 768], P('tensor', 'dp')
Inputs may be any that keep to these rules, and one draw needn't show every extreme that they name: `short_lengths`: the first short pair has 256 valid tokens. `long_lengths`: the first long pair has 512 valid tokens.
All inputs are finite; a program needn't handle non-finite values.
Results may differ from a plain program's by a relative error of at most 0.013.
The roundings to bfloat16 on the way count: a program that leaves them out, or rounds other values in their place, can miss the bound.
Values sent between devices are 32-bit elements; how exact they have to be, the bound alone decides.
No kernel may reach another device: no remote copies, remote signals or barrier semaphores. Data moves between devices by JAX's collectives and lax.ppermute only.
A program may use at most 128 MiB of HBM per device.

v0:
```python
import jax
import jax.numpy as jnp
from jax import lax
from jax.sharding import PartitionSpec as P

HD = 64


EPSILON = 1e-12


def normalize(hidden):
    center = hidden - jnp.mean(hidden, -1, keepdims=True)
    factor = lax.rsqrt(jnp.mean(center * center, -1, keepdims=True) + EPSILON)
    return (center * factor, factor[:, 0])


def norm_back(upstream, normed, factor, gain):
    scaled = upstream * gain
    inner_mean = jnp.mean(scaled, -1, keepdims=True)
    cross_mean = jnp.mean(scaled * normed, -1, keepdims=True)
    return factor[:, None] * (scaled - inner_mean - normed * cross_mean)


def gelu_exact(inner):
    return jax.nn.gelu(inner, approximate=False)


def masked_scores(queries, key_rows, length):
    scores = jnp.einsum(
        "qhe,khe->hqk", queries, key_rows, preferred_element_type=jnp.float32
    ) * HD ** (-0.5)
    visible = jnp.arange(key_rows.shape[0]) < length
    return jnp.where(visible[None, None, :], scores, -1e30)


def attend(queries, key_rows, value_rows, length):
    scores = masked_scores(queries, key_rows, length)
    largest = jnp.max(scores, -1, keepdims=True)
    weights_exp = jnp.exp(scores - largest)
    total = jnp.sum(weights_exp, -1, keepdims=True)
    probs = weights_exp / total
    mixed = jnp.einsum(
        "hqk,khe->qhe", probs.astype(jnp.bfloat16), value_rows, preferred_element_type=jnp.float32
    )
    log_total = largest[..., 0] + jnp.log(total[..., 0])
    return (mixed.astype(jnp.bfloat16), log_total)


def attend_back(queries, key_rows, value_rows, length, log_total, grad_mixed):
    scores = masked_scores(queries, key_rows, length)
    probs = jnp.exp(scores - log_total[..., None])
    grad_values = jnp.einsum(
        "hqk,qhe->khe", probs.astype(jnp.bfloat16), grad_mixed, preferred_element_type=jnp.float32
    )
    grad_probs = jnp.einsum(
        "qhe,khe->hqk", grad_mixed, value_rows, preferred_element_type=jnp.float32
    )
    centered = jnp.sum(probs * grad_probs, -1, keepdims=True)
    grad_scores = (probs * (grad_probs - centered)).astype(jnp.bfloat16)
    grad_queries = jnp.einsum(
        "hqk,khe->qhe", grad_scores, key_rows, preferred_element_type=jnp.float32
    ) * HD ** (-0.5)
    grad_keys = jnp.einsum(
        "hqk,qhe->khe", grad_scores, queries, preferred_element_type=jnp.float32
    ) * HD ** (-0.5)
    return (grad_queries, grad_keys, grad_values)


def forward_pair(item_tuple):
    pair_q, pair_k, pair_v, length = item_tuple
    return attend(pair_q, pair_k, pair_v, length)


def backward_pair(item_tuple):
    pair_q, pair_k, pair_v, length, pair_lse, pair_grad = item_tuple
    return attend_back(pair_q, pair_k, pair_v, length, pair_lse, pair_grad)


def on_device(
    short_tokens,
    short_lengths,
    long_tokens,
    long_lengths,
    w_qkv,
    b_qv,
    w_out,
    res_biases,
    ln_gains,
    ln_shifts,
    w_up,
    b_up,
    w_down,
    short_cotangent,
    long_cotangent,
):
    short_pairs, short_slot, model_width = short_tokens.shape
    long_pairs, long_slot = (long_tokens.shape[0], long_tokens.shape[1])
    short_rows = short_pairs * short_slot
    long_rows = long_pairs * long_slot
    local_width = w_qkv.shape[2]
    heads_here = b_qv.shape[1]
    head_size = b_qv.shape[2]
    flat = jnp.concatenate(
        [
            short_tokens.reshape(short_rows, model_width),
            long_tokens.reshape(long_rows, model_width),
        ],
        0,
    )
    flat_float = flat.astype(jnp.float32)
    gain_rows = ln_gains.astype(jnp.float32)
    shift_rows = ln_shifts.astype(jnp.float32)
    bias_float = res_biases.astype(jnp.float32)
    projected = jnp.einsum("rd,cde->cre", flat, w_qkv, preferred_element_type=jnp.float32)
    bias_rows = jnp.stack(
        [
            b_qv[0].reshape(local_width).astype(jnp.float32),
            jnp.zeros((local_width,), jnp.float32),
            b_qv[1].reshape(local_width).astype(jnp.float32),
        ]
    )
    projected = (projected + bias_rows[:, None, :]).astype(jnp.bfloat16)
    short_proj = projected[:, :short_rows].reshape(
        3, short_pairs, short_slot, heads_here, head_size
    )
    long_proj = projected[:, short_rows:].reshape(3, long_pairs, long_slot, heads_here, head_size)
    short_att, short_lse = lax.map(
        forward_pair, (short_proj[0], short_proj[1], short_proj[2], short_lengths)
    )
    long_att, long_lse = lax.map(
        forward_pair, (long_proj[0], long_proj[1], long_proj[2], long_lengths)
    )
    mixed = jnp.concatenate(
        [short_att.reshape(short_rows, local_width), long_att.reshape(long_rows, local_width)], 0
    )
    attn_part = jnp.dot(mixed, w_out, preferred_element_type=jnp.float32)
    attn_total = lax.psum(attn_part, "tensor")
    normed_one, factor_one = normalize(flat_float + attn_total + bias_float[0])
    first_out = normed_one * gain_rows[0] + shift_rows[0]
    first_low = first_out.astype(jnp.bfloat16)
    inner = jnp.dot(first_low, w_up, preferred_element_type=jnp.float32) + b_up[0].astype(
        jnp.float32
    )
    activated = gelu_exact(inner).astype(jnp.bfloat16)
    ffn_part = jnp.dot(activated, w_down, preferred_element_type=jnp.float32)
    ffn_total = lax.psum(ffn_part, "tensor")
    normed_two, factor_two = normalize(first_out + ffn_total + bias_float[1])
    encoded = (normed_two * gain_rows[1] + shift_rows[1]).astype(jnp.bfloat16)
    upstream = jnp.concatenate(
        [
            short_cotangent.reshape(short_rows, model_width),
            long_cotangent.reshape(long_rows, model_width),
        ],
        0,
    ).astype(jnp.float32)
    grad_second = norm_back(upstream, normed_two, factor_two, gain_rows[1])
    small_second = jnp.stack(
        [jnp.sum(grad_second, 0), jnp.sum(upstream * normed_two, 0), jnp.sum(upstream, 0)]
    )
    grad_branch = grad_second.astype(jnp.bfloat16)
    grad_down = jnp.einsum("rf,rd->fd", activated, grad_branch, preferred_element_type=jnp.float32)
    grad_activated = jnp.einsum(
        "rd,fd->rf", grad_branch, w_down, preferred_element_type=jnp.float32
    )
    ignored_value, gelu_pullback = jax.vjp(gelu_exact, inner)
    grad_inner = gelu_pullback(grad_activated)[0].astype(jnp.bfloat16)
    grad_up = jnp.einsum("rd,rf->df", first_low, grad_inner, preferred_element_type=jnp.float32)
    grad_up_bias = jnp.sum(grad_inner.astype(jnp.float32), 0)[None, :]
    input_part = jnp.einsum("rf,df->rd", grad_inner, w_up, preferred_element_type=jnp.float32)
    up_shard, down_shard, up_bias_shard, small_second_shard = (
        lax.psum_scatter(grad_up, "dp", scatter_dimension=0, tiled=True),
        lax.psum_scatter(grad_down, "dp", scatter_dimension=1, tiled=True),
        lax.psum_scatter(grad_up_bias, "dp", scatter_dimension=1, tiled=True),
        lax.psum_scatter(small_second, "dp", scatter_dimension=1, tiled=True),
    )
    grad_first_out = grad_second + lax.psum(input_part, "tensor")
    grad_first = norm_back(grad_first_out, normed_one, factor_one, gain_rows[0])
    small_first = jnp.stack(
        [
            jnp.sum(grad_first, 0),
            jnp.sum(grad_first_out * normed_one, 0),
            jnp.sum(grad_first_out, 0),
        ]
    )
    grad_attn = grad_first.astype(jnp.bfloat16)
    grad_out = jnp.einsum("rl,rd->ld", mixed, grad_attn, preferred_element_type=jnp.float32)
    grad_mixed = jnp.einsum(
        "rd,ld->rl", grad_attn, w_out, preferred_element_type=jnp.float32
    ).astype(jnp.bfloat16)
    short_grad_mixed = grad_mixed[:short_rows].reshape(
        short_pairs, short_slot, heads_here, head_size
    )
    long_grad_mixed = grad_mixed[short_rows:].reshape(long_pairs, long_slot, heads_here, head_size)
    short_gq, short_gk, short_gv = lax.map(
        backward_pair,
        (short_proj[0], short_proj[1], short_proj[2], short_lengths, short_lse, short_grad_mixed),
    )
    long_gq, long_gk, long_gv = lax.map(
        backward_pair,
        (long_proj[0], long_proj[1], long_proj[2], long_lengths, long_lse, long_grad_mixed),
    )
    short_grads = (
        jnp.stack([short_gq, short_gk, short_gv])
        .astype(jnp.bfloat16)
        .reshape(3, short_rows, local_width)
    )
    long_grads = (
        jnp.stack([long_gq, long_gk, long_gv])
        .astype(jnp.bfloat16)
        .reshape(3, long_rows, local_width)
    )
    grad_projected = jnp.concatenate([short_grads, long_grads], 1)
    grad_qkv = jnp.einsum("rd,cre->cde", flat, grad_projected, preferred_element_type=jnp.float32)
    grad_bias_rows = jnp.sum(grad_projected.astype(jnp.float32), 1)
    grad_qv_bias = jnp.stack([grad_bias_rows[0], grad_bias_rows[2]]).reshape(
        2, heads_here, head_size
    )
    token_part = jnp.einsum(
        "cre,cde->rd", grad_projected, w_qkv, preferred_element_type=jnp.float32
    )
    qkv_shard, qv_bias_shard, out_shard, small_first_shard = (
        lax.psum_scatter(grad_qkv, "dp", scatter_dimension=1, tiled=True),
        lax.psum_scatter(grad_qv_bias, "dp", scatter_dimension=2, tiled=True),
        lax.psum_scatter(grad_out, "dp", scatter_dimension=1, tiled=True),
        lax.psum_scatter(small_first, "dp", scatter_dimension=1, tiled=True),
    )
    grad_tokens = grad_first + lax.psum(token_part, "tensor")
    grad_res_biases = jnp.concatenate([small_first_shard[0:1], small_second_shard[0:1]], 0)
    grad_gains = jnp.concatenate([small_first_shard[1:2], small_second_shard[1:2]], 0)
    grad_shifts = jnp.concatenate([small_first_shard[2:3], small_second_shard[2:3]], 0)
    return (
        encoded[:short_rows].reshape(short_pairs, short_slot, model_width),
        encoded[short_rows:].reshape(long_pairs, long_slot, model_width),
        grad_tokens[:short_rows].reshape(short_pairs, short_slot, model_width),
        grad_tokens[short_rows:].reshape(long_pairs, long_slot, model_width),
        qkv_shard,
        qv_bias_shard,
        out_shard,
        grad_res_biases,
        grad_gains,
        grad_shifts,
        up_shard,
        up_bias_shard,
        down_shard,
    )


def solution(mesh):
    return jax.shard_map(
        on_device,
        mesh=mesh,
        in_specs=(
            P("dp", None, None),
            P("dp"),
            P("dp", None, None),
            P("dp"),
            P(None, None, "tensor"),
            P(None, "tensor", None),
            P("tensor", None),
            P(),
            P(),
            P(),
            P(None, "tensor"),
            P("tensor", None),
            P("tensor", None),
            P("dp", None, None),
            P("dp", None, None),
        ),
        out_specs=(
            P("dp", None, None),
            P("dp", None, None),
            P("dp", None, None),
            P("dp", None, None),
            P(None, "dp", "tensor"),
            P(None, "tensor", "dp"),
            P("tensor", "dp"),
            P(None, "dp"),
            P(None, "dp"),
            P(None, "dp"),
            P("dp", "tensor"),
            P("tensor", "dp"),
            P("tensor", "dp"),
        ),
        check_vma=False,
    )
```

profile of v0, /device:TPU:0, one launch (start us, length us, event | category | flops | bytes accessed | tf_op | source)
XLA Modules:
  0.0 1305.2 jit_solution(6530653363544916583)
XLA Ops:
  8.3 4.1 fusion.122
  15.2 2.1 squeeze.91
  21.0 15.0 %while.53 = (s32[]{:T(128)}, bf16[3,512,3,64]{1,3,2,0:T(8,128)(2,1)}, f32[3,3,512]{2,1,0:T(4,128)}, bf16[3,512,3,64]{1,3,2,0:T(8,128)(2,1)S(1)}, s32[3]{0:T(128)...) while((s32[]{:T(128)}, bf16[3,512,3,64]{1,3,2,0:T(8,128)(2,1)}, ...), condition=%wide.region_7.8_spmd, body=%wide.region_4.7_spmd.sunk | while | flops 210861056 | bytes 10283621 | solution.py:131
  24.4 1.6 fusion.200
  29.4 1.6 fusion.200
  34.4 1.6 fusion.200
  36.0 1.8 copy.104
  38.9 1.7 squeeze.88
  43.2 5.3 while.52
  50.9 4.7 fusion.137
  58.1 223.2 %all-reduce.6.cloned.1.call-done = f32[2048,768]{1,0:T(8,128)} async-done(((f32[2048,768]{1,0:T(8,128)}), f32[2048,768]{1,0:T(8,128)}) %all-reduce.6.cloned.1.call-update) | async-done | bytes 6291472 | tf_op jit(solution)/shard_map/psum | solution.py:138
  281.3 4.2 fusion.130
  288.2 18.4 %multiply_convert_fusion.2 = (bf16[2048,768]{1,0:T(8,128)(2,1)S(1)}, f32[2048,768]{1,0:T(8,128)}, f32[2048,768]{1,0:T(8,128)}) fusion(f32[768]{0:T(1024)S(1)} %copy-done.32, bf16[2048,768]{1,0:T(8,128)(2,1)S(1)} %fusion.103, bf16[768,768]{1,0:T(8,128)(2,1)S(1)} %copy-done), kind=kOutput, calls=%fused_computation.132 | convolution fusion | flops 2519728128 | bytes 20057088 | tf_op jit(solution)/shard_map/dot_general | solution.py:142
  306.6 1.7 copy-done.46
  308.3 4.6 fusion.138
  313.2 221.6 %all-reduce.8.cloned.1.call-done = f32[2048,768]{1,0:T(8,128)} async-done(((f32[2048,768]{1,0:T(8,128)}), f32[2048,768]{1,0:T(8,128)}) %all-reduce.8.cloned.1.call-update) | async-done | bytes 6291472 | tf_op jit(solution)/shard_map/psum | solution.py:147
  534.8 5.7 fusion.128
  542.4 4.6 fusion.97
  547.0 5.8 fusion.126
  552.9 9.5 convert_reduce_fusion.1
  562.4 1.8 copy-done.45
  564.2 4.5 fusion.139
  571.9 218.7 %all-reduce.10.cloned.1.call-done = f32[2048,768]{1,0:T(8,128)} async-done(((f32[2048,768]{1,0:T(8,128)}), f32[2048,768]{1,0:T(8,128)}) %all-reduce.10.cloned.1.call-update) | async-done | bytes 6291472 | tf_op jit(solution)/shard_map/psum | solution.py:177
  790.6 8.1 multiply_reduce_fusion.2
  798.8 4.7 fusion.125
  803.6 2.6 copy-done.3
  808.4 2.1 reshape.231
  811.8 25.9 %while.55 = (s32[]{:T(128)}, bf16[3,512,3,64]{1,3,2,0:T(8,128)(2,1)}, bf16[3,512,3,64]{1,3,2,0:T(8,128)(2,1)}, bf16[3,512,3,64]{1,3,2,0:T(8,128)(2,1)}, bf16[3,5...) while((s32[]{:T(128)}, ...), condition=%wide.region_24.25_spmd, body=%wide.region_22.24_spmd.sunk | while | flops 510589952 | bytes 35625200 | solution.py:199
  838.7 5.1 fusion.119
  844.2 9.6 while.54
  863.8 1.6 copy.118
  866.3 5.1 fusion.116
  871.3 4.3 copy.129
  875.6 4.7 reshape.242
  880.4 6.0 convolution_bitcast_fusion.1
  886.5 7.9 fusion.110
  894.7 7.0 fusion.140
  903.0 3.2 slice.147
  906.2 2.1 slice.146
  912.0 13.5 %all-reduce = f32[2,3,64]{2,1,0:T(4,128)S(1)} all-reduce(f32[2,3,64]{2,1,0:T(4,128)S(1)} %reshape.234), channel_id=3, replica_groups=mesh['dp'=8,'tensor'=4] {'dp'}, use_global_device_ids=true, to_apply=%region_28.29.clone | all-reduce | flops 384 | bytes 3072
  929.2 9.0 reduce-scatter.25.cloned.1.call-done
  938.2 1.6 copy.134
  939.8 42.0 %reduce-scatter.23.cloned.1.call-done = f32[96,576]{1,0:T(8,128)} async-done(((f32[768,576]{1,0:T(8,128)}), f32[96,576]{1,0:T(8,128)}) %reduce-scatter.23.cloned.1.call-update) | async-done | bytes 221200
  983.7 223.4 %all-reduce.12.cloned.1.call-done = f32[2048,768]{1,0:T(8,128)} async-done(((f32[2048,768]{1,0:T(8,128)}), f32[2048,768]{1,0:T(8,128)}) %all-reduce.12.cloned.1.call-update) | async-done | bytes 6291472 | tf_op jit(solution)/shard_map/psum | solution.py:228
  1207.0 5.5 add.175
  1212.5 2.5 slice.151
  1216.3 35.8 %reduce-scatter.21.cloned.1.call-done = f32[768,96]{0,1:T(8,128)} async-done(((f32[768,768]{0,1:T(8,128)}), f32[768,96]{0,1:T(8,128)}) %reduce-scatter.21.cloned.1.call-update) | async-done | bytes 294928 | tf_op jit(solution)/shard_map/reduce_scatter | solution.py:173
  1252.1 46.3 %reduce-scatter.19.cloned.1.call-done = f32[96,768]{1,0:T(8,128)} async-done(((f32[768,768]{1,0:T(8,128)}), f32[96,768]{1,0:T(8,128)}) %reduce-scatter.19.cloned.1.call-update) | async-done | bytes 294928 | tf_op jit(solution)/shard_map/reduce_scatter | solution.py:172
  (310 shorter events, 101.5 us)
Async XLA Ops:
  7.2 281.0 %copy-start = (bf16[768,768]{1,0:T(8,128)(2,1)S(1)}, bf16[768,768]{1,0:T(8,128)(2,1)}, u32[]{:S(2)}) copy-start(bf16[768,768]{1,0:T(8,128)(2,1)} %param.33) | copy-start | bytes 3538948
  7.2 274.1 %all-reduce.6.cloned.1.call-start = ((), (), s32[]{:S(2)}) async-start(), calls=%async_computation.7 | async-start | bytes 12582912 | tf_op jit(solution)/shard_map/psum | solution.py:138
  12.8 8.1 copy-start.40
  21.0 20.5 %copy-start.16 = (bf16[1,512,192]{1,2,0:T(8,128)(2,1)S(1)}, bf16[1,512,192]{1,2,0:T(8,128)(2,1)}, u32[]{:S(2)}) copy-start(bf16[1,512,192]{1,2,0:T(8,128)(2,1)} %get-tuple-element.455) | copy-start | bytes 589828
  21.0 22.1 %copy-start.42 = (s32[2]{0:T(128)S(1)}, s32[2]{0:T(128)}, u32[]{:S(2)}) copy-start(s32[2]{0:T(128)} %param.24) | copy-start | bytes 28
  36.0 7.1 copy-start.6
  48.5 7.1 copy-start.23
  50.9 5.0 copy-start.35
  50.9 5.4 copy-start.34
  55.6 479.2 %all-reduce.8.cloned.1.call-start = ((), (), s32[]{:S(2)}) async-start(), calls=%async_computation.8 | async-start | bytes 12582912 | tf_op jit(solution)/shard_map/psum | solution.py:147
  285.5 2.7 copy-start.2
  286.4 1.8 copy-start.32
  288.2 18.5 %copy-start.9 = (bf16[2048,768]{1,0:T(8,128)(2,1)}, bf16[2048,768]{1,0:T(8,128)(2,1)S(1)}, u32[]{:S(2)}) copy-start(bf16[2048,768]{1,0:T(8,128)(2,1)S(1)} %fusion.103) | copy-start | bytes 9437188
  288.2 20.2 %copy-start.38 = (bf16[768,768]{1,0:T(8,128)(2,1)S(1)}, bf16[768,768]{1,0:T(8,128)(2,1)}, u32[]{:S(2)}) copy-start(bf16[768,768]{1,0:T(8,128)(2,1)} %param.35) | copy-start | bytes 3538948
  312.9 477.7 %all-reduce.10.cloned.1.call-start = ((), (), s32[]{:S(2)}) async-start(), calls=%async_computation.9 | async-start | bytes 12582912 | tf_op jit(solution)/shard_map/psum | solution.py:177
  540.6 1.8 copy-start.7
  540.6 1.8 copy-start.25
  541.5 5.5 copy-start.29
  542.4 10.5 slice-start.1
  547.0 5.9 copy-start.33
  547.0 5.9 copy-start.39
  547.0 5.9 slice-start.2
  552.9 9.5 copy-start.4
  562.4 1.8 copy-start.45
  568.7 221.9 %copy-start.22 = (f32[768]{0:T(1024)S(1)}, f32[768]{0:T(1024)}, u32[]{:S(2)}) copy-start(f32[768]{0:T(1024)} %get-tuple-element.469) | copy-start | bytes 9220
  568.7 339.5 %reduce-scatter.31.cloned.1.call-start = ((), (), s32[]{:S(2)}) async-start(), calls=%async_computation.17 | async-start | bytes 442368
  570.3 339.3 %reduce-scatter.29.cloned.1.call-start = ((), (), s32[]{:S(2)}) async-start(), calls=%async_computation.16 | async-start | bytes 442368
  571.4 354.8 %reduce-scatter.27.cloned.1.call-start = ((), (), s32[]{:S(2)}) async-start(), calls=%async_computation.15 | async-start | bytes 442368
  798.8 7.4 copy-start.12
  803.5 2.7 copy-start.3
  803.5 8.3 copy-start.41
  815.3 2.0 copy-start.19
  823.9 2.0 copy-start.19
  832.5 2.0 copy-start.19
  837.7 6.1 slice-start
  837.7 6.5 copy-start.11
  837.7 6.5 copy-start.24
  837.7 6.5 copy-start.43
  838.7 99.5 %reduce-scatter.25.cloned.1.call-start = ((), (), s32[]{:S(2)}) async-start(), calls=%async_computation.14 | async-start | bytes 884736
  843.9 137.9 %reduce-scatter.23.cloned.1.call-start = ((), (), s32[]{:S(2)}) async-start(), calls=%async_computation.13 | async-start | bytes 2211840
  853.8 12.5 copy-start.13
  871.3 9.0 copy-start.14
  871.3 9.1 copy-start.15
  880.3 326.7 %all-reduce.12.cloned.1.call-start = ((), (), s32[]{:S(2)}) async-start(), calls=%async_computation.10 | async-start | bytes 12582912 | tf_op jit(solution)/shard_map/psum | solution.py:228
  886.4 365.6 %reduce-scatter.21.cloned.1.call-start = ((), (), s32[]{:S(2)}) async-start(), calls=%async_computation.12 | async-start | bytes 2654208 | tf_op jit(solution)/shard_map/reduce_scatter | solution.py:173
  894.4 7.3 copy-start.44
  894.5 404.0 %reduce-scatter.19.cloned.1.call-start = ((), (), s32[]{:S(2)}) async-start(), calls=%async_computation.11 | async-start | bytes 2654208 | tf_op jit(solution)/shard_map/reduce_scatter | solution.py:172
  1207.0 91.4 %copy-start.1 = (bf16[768,768]{1,0:T(8,128)(2,1)S(1)}, bf16[768,768]{1,0:T(8,128)(2,1)}, u32[]{:S(2)}) copy-start(bf16[768,768]{1,0:T(8,128)(2,1)} %param.33) | copy-start | bytes 3538948
  (21 other events, 22.3 us)
Sparse Core Ops, SparseCore 0:
  55.7 225.5 all-reduce.5
  313.0 221.7 all-reduce.7
  568.9 221.7 all-reduce.9
  793.5 32.7 reduce-scatter.30
  829.3 33.9 reduce-scatter.28
  866.1 33.8 reduce-scatter.26
  903.2 34.9 reduce-scatter.24
  941.6 40.1 reduce-scatter.22
  984.2 222.8 all-reduce.11
  1210.8 41.2 reduce-scatter.20
  1256.0 42.3 reduce-scatter.18
where the time goes:
time: 1310 us
  waiting for transfers between devices  1020 us (78%)
  matrix products  109 us (8%)
  local copies, waits for them, and re-layouts  84.6 us (6%)
  other arithmetic  59.6 us (5%)
  between operations  15.6 us (1%)
  blocking collectives  13.5 us (1%)
    psum x1, waiting for transfers between devices, on_device(): grad_tokens = grad_first + lax.psum(token_part, 'tensor')  223 us
    psum x1, waiting for transfers between devices, on_device(): attn_total = lax.psum(attn_part, 'tensor')  223 us
    psum x1, waiting for transfers between devices, on_device(): ffn_total = lax.psum(ffn_part, 'tensor')  222 us
    psum x1, waiting for transfers between devices, on_device(): grad_first_out = grad_second + lax.psum(input_part, 'tensor')  219 us
    unnamed x16, waiting for transfers between devices  51.1 us
    reduce_scatter x1, waiting for transfers between devices, on_device(): lax.psum_scatter(grad_up, 'dp', scatter_dimension=0, tiled=True)  46.3 us
    reduce_scatter x1, waiting for transfers between devices, on_device(): lax.psum_scatter(grad_down, 'dp', scatter_dimension=1, tiled=True)  35.8 us
    unnamed x111, local copies, waits for them, and re-layouts  28.2 us
  transfers between devices with their start and end apart: 11, of which 8 were waited for; matrix products, arithmetic and copies ran while one was open for 10% of the time, Pallas kernels for 0%

commit v1 on v0

v1 whole, which is shorter than its diff:
```python
import jax
import jax.numpy as jnp
import numpy as np
from jax import lax
from jax.experimental import pallas as pl
from jax.experimental.pallas import tpu as pltpu
from jax.sharding import PartitionSpec as P

HD = 64
EPS = 1e-12
BF = jnp.bfloat16
F32 = jnp.float32
NT = (((1,), (1,)), ((), ()))
TN = (((0,), (0,)), ((), ()))


def dot(a, b, dims=(((1,), (0,)), ((), ()))):
    return lax.dot_general(a, b, dims, preferred_element_type=F32)


def lanes(width, test):
    lane = lax.broadcasted_iota(jnp.int32, (1, width), 1)
    return jnp.where(test(lane), 1.0, 0.0).astype(F32)


def head_row(h, width, extra):
    w = width * HD

    def test(lane):
        own = (lane >= h * HD) & (lane < (h + 1) * HD)
        if extra:
            own = own | ((lane >= w + 1 + 3 * h) & (lane < w + 4 + 3 * h))
        return own

    return test


def split3(x):
    hi = x.astype(BF).astype(F32)
    rest = x - hi
    mid = rest.astype(BF).astype(F32)
    return hi, mid, rest - mid


def attn_fwd_kernel(
    sp_ref, len_ref, x_ref, w_ref, b_ref, *refs, nshort, short_slot, heads, blk
):
    p_ref, o_ref, w_s = refs[-3:]
    hw = heads * HD
    g, b = pl.program_id(0), pl.program_id(1)
    sub = blk // short_slot
    long0 = nshort // sub

    @pl.when(b == 0)
    def _():
        w_s[...] = jnp.zeros_like(w_s)
        for c in range(3):
            w_s[256 * c : 256 * c + hw] = w_ref[0, c * hw : (c + 1) * hw].astype(BF)

    p_ref[0] = (dot(x_ref[...], w_s[...], NT) + b_ref[0]).astype(BF)

    def pair(row, rows, length):
        sl = pl.ds(row, rows)
        pos = lax.broadcasted_iota(jnp.int32, (rows, 1), 0)
        hidden = jnp.where(pos < length, 0.0, -1e30)
        at_mask = lanes(256, lambda l: l == hw)
        q = (p_ref[0, sl, 0:256].astype(F32) * 0.125 + at_mask).astype(BF)
        k = (p_ref[0, sl, 256:512].astype(F32) + hidden * at_mask).astype(BF)
        v = p_ref[0, sl, 512:768]
        p_ref[0, sl, 256:512] = k
        out = jnp.zeros((rows, 256), F32)
        ext = jnp.zeros((rows, 256), F32)
        for h in range(heads):
            own = lanes(256, head_row(h, heads, False))
            s = dot(q * (own + at_mask).astype(BF), k, NT)
            m = jnp.max(s, axis=1, keepdims=True)
            e = jnp.exp(s - m)
            total = jnp.sum(e, axis=1, keepdims=True)
            a = (e * (1.0 / total)).astype(BF)
            out = out + dot(a, v * own.astype(BF))
            for i, part in enumerate(split3(-(m + jnp.log(total)))):
                ext = ext + part * lanes(256, lambda l: l == hw + 1 + 3 * h + i)
        p_ref[0, sl, 0:256] = (q.astype(F32) + ext).astype(BF)
        o_ref[0, sl] = out.astype(BF)

    @pl.when(b < long0)
    def _():
        for i in range(sub):
            pair(i * short_slot, short_slot, len_ref[b * sub + i])

    @pl.when(b >= long0)
    def _():
        pair(0, blk, len_ref[nshort + b - long0])


def attn_fwd(groups, lens, x, w, bias, prev, nshort, short_slot, heads, blk, w_index):
    rows, d = x.shape
    nb = rows // blk
    tensor = bias.shape[0]
    n = groups.shape[0]
    wrows = 3 * heads * HD

    def out_map(g, b, sp, ln):
        return (sp[g], b, 0)

    in_specs = [
        pl.BlockSpec((blk, d), lambda g, b, sp, ln: (b, 0)),
        pl.BlockSpec((1, wrows, d), lambda g, b, sp, ln: (w_index(g, sp), 0, 0)),
        pl.BlockSpec((1, 1, 768), lambda g, b, sp, ln: (sp[g], 0, 0)),
    ]
    args = [x, w, bias]
    aliases = {}
    if prev is not None:
        in_specs += [pl.BlockSpec(memory_space=pl.ANY)] * 2
        args += list(prev)
        aliases = {5: 0, 6: 1}
    return pl.pallas_call(
        lambda *r: attn_fwd_kernel(
            *r, nshort=nshort, short_slot=short_slot, heads=heads, blk=blk
        ),
        grid_spec=pltpu.PrefetchScalarGridSpec(
            num_scalar_prefetch=2,
            grid=(n, nb),
            in_specs=in_specs,
            out_specs=[
                pl.BlockSpec((1, blk, 768), out_map),
                pl.BlockSpec((1, blk, 256), out_map),
            ],
            scratch_shapes=[pltpu.VMEM((768, d), BF)],
        ),
        out_shape=[
            jax.ShapeDtypeStruct((tensor, rows, 768), BF),
            jax.ShapeDtypeStruct((tensor, rows, 256), BF),
        ],
        input_output_aliases=aliases,
        compiler_params=pltpu.CompilerParams(vmem_limit_bytes=60 * 2**20),
        name="attn_fwd",
    )(groups, lens, *args)


def attn_bwd_pair(refs, sl, rows, heads):
    p_ref, o_ref, do_ref = refs
    hw = heads * HD
    q, k, v = p_ref[0, sl, 0:256], p_ref[0, sl, 256:512], p_ref[0, sl, 512:768]
    do = do_ref[0, sl]
    do32 = do.astype(F32)
    prod = do32 * o_ref[0, sl].astype(F32)
    ext = do32
    for h in range(heads):
        own = lanes(256, head_row(h, heads, False))
        delta = jnp.sum(prod * own, axis=1, keepdims=True)
        for i, part in enumerate(split3(-delta)):
            ext = ext + part * lanes(256, lambda l: l == hw + 1 + 3 * h + i)
    do_ext = ext.astype(BF)
    kt = k.T
    at_mask = lanes(256, lambda l: l == hw)
    dk = jnp.zeros((rows, 256), F32)
    dv = jnp.zeros((rows, 256), F32)
    dqs = []
    for h in range(heads):
        row = lanes(256, head_row(h, heads, True))
        qh = q * (row + at_mask).astype(BF)
        doh = do_ext * row.astype(BF)
        p = jnp.exp(dot(k, qh, NT))
        ds = (p * dot(v, doh, NT)).astype(BF)
        dv = dv + dot(p.astype(BF), doh)
        dk = dk + dot(ds, qh)
        dqs.append(dot(kt[h * HD : (h + 1) * HD], ds))
    dqs.append(jnp.zeros((256 - hw, rows), F32))
    dq = jnp.concatenate(dqs, 0).T * 0.125
    real = lanes(256, lambda l: l < hw)
    return dq.astype(BF), (dk * real).astype(BF), (dv * real).astype(BF)


def over_pairs(b, refs, dst, *, nshort, short_slot, heads, blk):
    sub = blk // short_slot
    long0 = nshort // sub

    def one(row, rows):
        sl = pl.ds(row, rows)
        for c, val in enumerate(attn_bwd_pair(refs, sl, rows, heads)):
            dst(sl, c, val)

    @pl.when(b < long0)
    def _():
        for i in range(sub):
            one(i * short_slot, short_slot)

    @pl.when(b >= long0)
    def _():
        one(0, blk)


def bwd_own_kernel(sp_ref, x_ref, p_ref, o_ref, do_ref, dp_ref, gw_ref, gb_ref, **kw):
    b = pl.program_id(0)

    def dst(sl, c, val):
        dp_ref[sl, 256 * c : 256 * (c + 1)] = val

    over_pairs(b, (p_ref, o_ref, do_ref), dst, **kw)
    dp = dp_ref[...]
    gw = dot(x_ref[...], dp, TN)
    gb = jnp.sum(dp.astype(F32).reshape(-1, 8, 768), axis=0)

    @pl.when(b == 0)
    def _():
        gw_ref[...] = gw
        gb_ref[...] = gb

    @pl.when(b > 0)
    def _():
        gw_ref[...] += gw
        gb_ref[...] += gb


def bwd_own(own, x, p, o, do, blk, **kw):
    rows, d = x.shape
    return pl.pallas_call(
        lambda *r: bwd_own_kernel(*r, blk=blk, **kw),
        grid_spec=pltpu.PrefetchScalarGridSpec(
            num_scalar_prefetch=1,
            grid=(rows // blk,),
            in_specs=[
                pl.BlockSpec((blk, d), lambda b, sp: (b, 0)),
                pl.BlockSpec((1, blk, 768), lambda b, sp: (sp[0], b, 0)),
                pl.BlockSpec((1, blk, 256), lambda b, sp: (sp[0], b, 0)),
                pl.BlockSpec((1, blk, 256), lambda b, sp: (sp[0], b, 0)),
            ],
            out_specs=[
                pl.BlockSpec((blk, 768), lambda b, sp: (b, 0)),
                pl.BlockSpec((d, 768), lambda b, sp: (0, 0)),
                pl.BlockSpec((8, 768), lambda b, sp: (0, 0)),
            ],
        ),
        out_shape=[
            jax.ShapeDtypeStruct((rows, 768), BF),
            jax.ShapeDtypeStruct((d, 768), F32),
            jax.ShapeDtypeStruct((8, 768), F32),
        ],
        compiler_params=pltpu.CompilerParams(vmem_limit_bytes=60 * 2**20),
        name="attn_bwd_own",
    )(own, x, p, o, do)


def bwd_rest_kernel(sp_ref, p_ref, o_ref, do_ref, own_ref, dh_ref, w_ref, gx_ref, dp_s, w_s, **kw):
    b, g = pl.program_id(0), pl.program_id(1)
    tensor = w_s.shape[0]
    hw = kw["heads"] * HD
    me = sp_ref[0]
    grp = sp_ref[1 + g]

    @pl.when((b == 0) & (g == 0))
    def _():
        w_s[...] = jnp.zeros_like(w_s)
        for j in range(tensor):
            for c in range(3):
                w_s[j, 256 * c : 256 * c + hw] = w_ref[j, c * hw : (c + 1) * hw].astype(BF)

    @pl.when(g == 0)
    def _():
        dp_s[me] = own_ref[...]

    def dst(sl, c, val):
        dp_s[grp, sl, 256 * c : 256 * (c + 1)] = val

    over_pairs(b, (p_ref, o_ref, do_ref), dst, **kw)

    @pl.when(g == tensor - 2)
    def _():
        acc = dh_ref[...]
        for j in range(tensor):
            acc = acc + dot(dp_s[j], w_s[j])
        gx_ref[...] = acc


def bwd_rest(sp, p, o, do, own_dp, dh, w, blk, **kw):
    tensor, rows, _ = p.shape
    d = dh.shape[1]
    wrows = 3 * kw["heads"] * HD

    def grp_map(b, g, sp):
        return (sp[1 + g], b, 0)

    return pl.pallas_call(
        lambda *r: bwd_rest_kernel(*r, blk=blk, **kw),
        grid_spec=pltpu.PrefetchScalarGridSpec(
            num_scalar_prefetch=1,
            grid=(rows // blk, tensor - 1),
            in_specs=[
                pl.BlockSpec((1, blk, 768), grp_map),
                pl.BlockSpec((1, blk, 256), grp_map),
                pl.BlockSpec((1, blk, 256), grp_map),
                pl.BlockSpec((blk, 768), lambda b, g, sp: (b, 0)),
                pl.BlockSpec((blk, d), lambda b, g, sp: (b, 0)),
                pl.BlockSpec((tensor, wrows, d), lambda b, g, sp: (0, 0, 0), pipeline_mode=pl.Buffered(1)),
            ],
            out_specs=pl.BlockSpec((blk, d), lambda b, g, sp: (b, 0)),
            scratch_shapes=[
                pltpu.VMEM((tensor, blk, 768), BF),
                pltpu.VMEM((tensor, 768, d), BF),
            ],
        ),
        out_shape=jax.ShapeDtypeStruct((rows, d), F32),
        compiler_params=pltpu.CompilerParams(vmem_limit_bytes=60 * 2**20),
        name="attn_bwd_rest",
    )(sp, p, o, do, own_dp, dh, w)


def norm_stats(h):
    center = h - jnp.mean(h, -1, keepdims=True)
    rstd = lax.rsqrt(jnp.mean(center * center, -1, keepdims=True) + EPS)
    return center * rstd, rstd


def norm_back(dy, xhat, rstd, gain):
    s = dy * gain
    return rstd * (
        s - jnp.mean(s, -1, keepdims=True) - xhat * jnp.mean(s * xhat, -1, keepdims=True)
    )


def gelu_both(u):
    phi = 0.5 + 0.5 * lax.erf(u * 0.7071067811865476)
    pdf = jnp.exp2(u * u * (-0.5 * 1.4426950408889634)) * 0.3989422804014327
    return u * phi, phi + u * pdf


def row8(x):
    return jnp.sum(x.reshape(-1, 8, x.shape[-1]), axis=0)


def ffn_kernel(
    sp_ref,
    x_ref,
    cot_ref,
    o_ref,
    vec_ref,
    bup_ref,
    wo_hbm,
    wu_hbm,
    wd_hbm,
    enc_ref,
    dh_ref,
    do_ref,
    gu_ref,
    gd_ref,
    go_ref,
    sm_ref,
    wo_s,
    wu_s,
    wd_s,
    stage,
    sems,
    g_s,
    gp_s,
    du_s,
    *,
    wo_row,
):
    i = pl.program_id(0)
    me = sp_ref[0]
    tensor, hw = wu_s.shape[0], wo_hbm.shape[1] - wo_row

    @pl.when(i == 0)
    def _():
        work = []
        for j in range(tensor):
            work.append((wo_hbm.at[j, pl.ds(wo_row, hw)], hw, wo_s, j))
        for j in range(tensor):
            work.append((wu_hbm.at[j], 768, wu_s, j))
        for j in range(tensor):
            work.append((wd_hbm.at[j], 768, wd_s, j))

        def copy(n):
            src, r, _, _ = work[n]
            return pltpu.make_async_copy(src, stage.at[n % 3, pl.ds(0, r)], sems.at[n % 3])

        copy(0).start()
        copy(1).start()
        wo_s[...] = jnp.zeros_like(wo_s)
        gu_ref[...] = jnp.zeros_like(gu_ref)
        gd_ref[...] = jnp.zeros_like(gd_ref)
        go_ref[...] = jnp.zeros_like(go_ref)
        sm_ref[...] = jnp.zeros_like(sm_ref)
        for n in range(len(work)):
            if n + 2 < len(work):
                copy(n + 2).start()
            copy(n).wait()
            _, r, dst, j = work[n]
            dst[j, 0:r] = stage[n % 3, 0:r].astype(BF)

    def vec(n):
        return vec_ref[n : n + 1].astype(F32)

    attn = dot(o_ref[0], wo_s[0])
    for j in range(1, tensor):
        attn = attn + dot(o_ref[j], wo_s[j])
    xhat1, rstd1 = norm_stats(x_ref[...].astype(F32) + attn + vec(0))
    y1 = xhat1 * vec(2) + vec(4)
    y1b = y1.astype(BF)
    ffn = jnp.zeros_like(y1)
    for j in range(tensor):
        u = dot(y1b, wu_s[j]) + bup_ref[j : j + 1]
        g, gp = gelu_both(u)
        gb = g.astype(BF)
        g_s[j] = gb
        gp_s[j] = gp
        ffn = ffn + dot(gb, wd_s[j])
    xhat2, rstd2 = norm_stats(y1 + ffn + vec(1))
    enc_ref[...] = (xhat2 * vec(3) + vec(5)).astype(BF)
    dy = cot_ref[...].astype(F32)
    dh2 = norm_back(dy, xhat2, rstd2, vec(3))
    dz = dh2.astype(BF)
    sm_ref[1] += row8(dh2)
    sm_ref[3] += row8(dy * xhat2)
    sm_ref[5] += row8(dy)
    dy1 = dh2
    for j in range(tensor):
        du = (dot(dz, wd_s[j], NT) * gp_s[j]).astype(BF)
        du_s[j] = du
        dy1 = dy1 + dot(du, wu_s[j], NT)
    du_own = du_s[me]
    gu_ref[...] += dot(y1b, du_own, TN)
    gd_ref[...] += dot(dz, g_s[me], TN)
    sm_ref[6] += row8(du_own.astype(F32))
    dh1 = norm_back(dy1, xhat1, rstd1, vec(2))
    dh_ref[...] = dh1
    da = dh1.astype(BF)
    sm_ref[0] += row8(dh1)
    sm_ref[2] += row8(dy1 * xhat1)
    sm_ref[4] += row8(dy1)
    go_ref[...] += dot(da, o_ref[me], TN)
    for j in range(tensor):
        do_ref[j] = dot(da, wo_s[j], NT).astype(BF)


def ffn_block(sp, x, cot, o, vecs, bup, w1, wu, wd, wo_row, blk):
    rows, d = x.shape
    tensor = o.shape[0]
    fl = wu.shape[2]
    row = lambda i, sp: (i, 0)
    grp = lambda i, sp: (0, i, 0)
    const = lambda i, sp: (0, 0)
    return pl.pallas_call(
        lambda *r: ffn_kernel(*r, wo_row=wo_row),
        grid_spec=pltpu.PrefetchScalarGridSpec(
            num_scalar_prefetch=1,
            grid=(rows // blk,),
            in_specs=[
                pl.BlockSpec((blk, d), row),
                pl.BlockSpec((blk, d), row),
                pl.BlockSpec((tensor, blk, 256), grp),
                pl.BlockSpec((8, d), const),
                pl.BlockSpec((tensor, fl), const),
                pl.BlockSpec(memory_space=pl.ANY),
                pl.BlockSpec(memory_space=pl.ANY),
                pl.BlockSpec(memory_space=pl.ANY),
            ],
            out_specs=[
                pl.BlockSpec((blk, d), row),
                pl.BlockSpec((blk, d), row),
                pl.BlockSpec((tensor, blk, 256), grp),
                pl.BlockSpec((d, fl), const, pipeline_mode=pl.Buffered(1)),
                pl.BlockSpec((d, fl), const, pipeline_mode=pl.Buffered(1)),
                pl.BlockSpec((d, 256), const, pipeline_mode=pl.Buffered(1)),
                pl.BlockSpec((8, 8, d), lambda i, sp: (0, 0, 0)),
            ],
            scratch_shapes=[
                pltpu.VMEM((tensor, 256, d), BF),
                pltpu.VMEM((tensor, d, fl), BF),
                pltpu.VMEM((tensor, fl, d), BF),
                pltpu.VMEM((3, 768, 768), F32),
                pltpu.SemaphoreType.DMA((3,)),
                pltpu.VMEM((tensor, blk, fl), BF),
                pltpu.VMEM((tensor, blk, fl), F32),
                pltpu.VMEM((tensor, blk, fl), BF),
            ],
        ),
        out_shape=[
            jax.ShapeDtypeStruct((rows, d), BF),
            jax.ShapeDtypeStruct((rows, d), F32),
            jax.ShapeDtypeStruct((tensor, rows, 256), BF),
            jax.ShapeDtypeStruct((d, fl), F32),
            jax.ShapeDtypeStruct((d, fl), F32),
            jax.ShapeDtypeStruct((d, 256), F32),
            jax.ShapeDtypeStruct((8, 8, d), F32),
        ],
        compiler_params=pltpu.CompilerParams(vmem_limit_bytes=62 * 2**20),
        name="ffn_block",
    )(sp, x, cot, o, vecs, bup, w1, wu, wd)


def gather(shard, n_dp, n_tensor):
    r = shard.shape[0] // n_dp
    piece = lax.dynamic_slice_in_dim(shard, lax.axis_index("dp") * r, r, 0).astype(F32)
    full = lax.all_gather(piece, ("tensor", "dp"), axis=0, tiled=True)
    return full.reshape(n_tensor, shard.shape[0], shard.shape[1])


def make(n_dp, n_tensor):
    def on_device(
        short_tokens,
        short_lengths,
        long_tokens,
        long_lengths,
        w_qkv,
        b_qv,
        w_out,
        res_biases,
        ln_gains,
        ln_shifts,
        w_up,
        b_up,
        w_down,
        short_cotangent,
        long_cotangent,
    ):
        ns, ss, d = short_tokens.shape
        nl, ls, _ = long_tokens.shape
        srows = ns * ss
        rows = srows + nl * ls
        heads, hd = b_qv.shape[1], b_qv.shape[2]
        hw = heads * hd
        blk = ls
        kw = dict(nshort=ns, short_slot=ss, heads=heads, blk=blk)
        me = lax.axis_index("tensor").astype(jnp.int32)
        rest = (me + 1 + jnp.arange(n_tensor - 1, dtype=jnp.int32)) % n_tensor

        w1_own = jnp.concatenate([w_qkv.transpose(0, 2, 1).reshape(3 * hw, d), w_out], 0)
        w1 = gather(w1_own, n_dp, n_tensor)
        wu = gather(w_up, n_dp, n_tensor)
        wd = gather(w_down, n_dp, n_tensor)
        small = jnp.concatenate([b_qv.reshape(2 * hw), b_up.reshape(-1)]).astype(F32)
        small = lax.all_gather(small, "tensor", axis=0)
        bqv = small[:, : 2 * hw].reshape(n_tensor, 2, hw)
        bup = small[:, 2 * hw :]
        one = np.zeros((1, 256 - hw), np.float32)
        one[:, 1 : 1 + 3 * heads] = 1.0
        pad1 = jnp.broadcast_to(jnp.asarray(one), (n_tensor, 256 - hw))
        zero = jnp.zeros((n_tensor, 256 - hw), F32)
        bias = jnp.concatenate(
            [bqv[:, 0], zero, jnp.zeros((n_tensor, hw), F32), pad1, bqv[:, 1], pad1], 1
        ).reshape(n_tensor, 1, 768)

        x = jnp.concatenate([short_tokens.reshape(srows, d), long_tokens.reshape(-1, d)], 0)
        cot = jnp.concatenate(
            [short_cotangent.reshape(srows, d), long_cotangent.reshape(-1, d)], 0
        )
        lens = jnp.concatenate([short_lengths, long_lengths])
        own = me.reshape(1)
        own_first = attn_fwd(
            own, lens, x, w1_own[None], bias, None, w_index=lambda g, sp: 0, **kw
        )
        p, o = attn_fwd(rest, lens, x, w1, bias, own_first, w_index=lambda g, sp: sp[g], **kw)
        vecs = jnp.concatenate([res_biases, ln_gains, ln_shifts, jnp.zeros((2, d), BF)], 0).astype(F32)
        enc, dh, do, gu, gd, go, sm = ffn_block(
            own, x, cot, o, vecs, bup, w1, wu, wd, 3 * hw, 256
        )
        sm = sm.sum(1)
        up_shard = lax.psum_scatter(gu, "dp", scatter_dimension=0, tiled=True)
        down_shard = lax.psum_scatter(gd, "dp", scatter_dimension=0, tiled=True).T
        out_shard = lax.psum_scatter(go[:, :hw], "dp", scatter_dimension=0, tiled=True).T
        small_shard = lax.psum_scatter(sm, "dp", scatter_dimension=1, tiled=True)
        dp_own, gw, gb = bwd_own(own, x, p, o, do, **kw)
        gx = bwd_rest(jnp.concatenate([own, rest]), p, o, do, dp_own, dh, w1, **kw)
        gw = gw.reshape(d, 3, 256)[:, :, :hw].reshape(d, 3 * hw)
        gw = lax.psum_scatter(gw, "dp", scatter_dimension=0, tiled=True)
        gqkv = gw.reshape(-1, 3, hw).transpose(1, 0, 2)
        gb = gb.sum(0).reshape(3, 256)
        gb = jnp.stack([gb[0, :hw], gb[2, :hw]]).reshape(2, heads, hd)
        qv_shard = lax.psum_scatter(gb, "dp", scatter_dimension=2, tiled=True)
        return (
            enc[:srows].reshape(ns, ss, d),
            enc[srows:].reshape(nl, ls, d),
            gx[:srows].reshape(ns, ss, d),
            gx[srows:].reshape(nl, ls, d),
            gqkv,
            qv_shard,
            out_shard,
            small_shard[0:2],
            small_shard[2:4],
            small_shard[4:6],
            up_shard,
            small_shard[6:7],
            down_shard,
        )

    return on_device


def solution(mesh):
    tok = P("dp", None, None)
    return jax.shard_map(
        make(mesh.shape["dp"], mesh.shape["tensor"]),
        mesh=mesh,
        in_specs=(
            tok,
            P("dp"),
            tok,
            P("dp"),
            P(None, None, "tensor"),
            P(None, "tensor", None),
            P("tensor", None),
            P(),
            P(),
            P(),
            P(None, "tensor"),
            P("tensor", None),
            P("tensor", None),
            tok,
            tok,
        ),
        out_specs=(
            tok,
            tok,
            tok,
            tok,
            P(None, "dp", "tensor"),
            P(None, "tensor", "dp"),
            P("tensor", "dp"),
            P(None, "dp"),
            P(None, "dp"),
            P(None, "dp"),
            P("dp", "tensor"),
            P("tensor", "dp"),
            P("tensor", "dp"),
        ),
        check_vma=False,
    )
```

time: 1310 us -> 559 us (0.43)
  waiting for transfers between devices: 1020 us -> 268 us
  Pallas kernels: 0 us -> 204 us
  matrix products: 109 us -> 0 us
  local copies, waits for them, and re-layouts: 84.6 us -> 28.5 us
  other arithmetic: 59.6 us -> 14.8 us
  blocking collectives: 13.5 us -> 28.3 us
    psum x4 -> x0, waiting for transfers between devices: 887 us -> none  [the longest x1 223 us: on_device(): grad_tokens = grad_first + lax.psum(token_part, 'tensor')]
    pallas_call x0 -> x5, Pallas kernels: none -> 204 us  [the longest x1 80.1 us: ffn_block(): pl.pallas_call(lambda *r: ffn_kernel(*r, wo_row=wo_row), grid_spec=pltpu....]
    all_gather x0 -> x3, waiting for transfers between devices: none -> 171 us  [gather(): full = lax.all_gather(piece, ('tensor', 'dp'), axis=0, tiled=True)]
    dot_general x45 -> x0, matrix products: 100 us -> none  [the longest x1 18.4 us: on_device(): jnp.dot(first_low, w_up, preferred_element_type=jnp.float32)]
    unnamed x16 -> x10, waiting for transfers between devices: 51.1 us -> 5.92 us
    reduce_sum x14 -> x2, other arithmetic: 38.2 us -> 0.99 us  [the longest x1 0.98 us: on_device(): sm = sm.sum(1)]
    unnamed x111 -> x44, local copies, waits for them, and re-layouts: 28.2 us -> 11.1 us
    all_gather x0 -> x1, blocking collectives: none -> 14.9 us  [on_device(): small = lax.all_gather(small, 'tensor', axis=0)]
  transfers between devices with their start and end apart: 11 -> 8, of which waited for: 8 -> 6; matrix products, arithmetic and copies ran while one was open for 10% -> 7% of each run, Pallas kernels for 0% -> 22%
where the time goes in v1:
time: 559 us
  waiting for transfers between devices  268 us (48%)
  Pallas kernels  204 us (36%)
  local copies, waits for them, and re-layouts  28.5 us (5%)
  blocking collectives  28.3 us (5%)
  between operations  15 us (3%)
  other arithmetic  14.8 us (3%)
    all_gather x3, waiting for transfers between devices, gather(): full = lax.all_gather(piece, ('tensor', 'dp'), axis=0, tiled=True)  171 us
    pallas_call x1, Pallas kernels, ffn_block(): pl.pallas_call(lambda *r: ffn_kernel(*r, wo_row=wo_row), grid_spec=pltpu....  80.1 us
    pallas_call x2, Pallas kernels, attn_fwd(): pl.pallas_call(lambda *r: attn_fwd_kernel(*r, nshort=nshort, short_slot=s...  54.3 us
    pallas_call x1, Pallas kernels, bwd_rest(): pl.pallas_call(lambda *r: bwd_rest_kernel(*r, blk=blk, **kw), grid_spec=p...  51 us
    reduce_scatter x1, waiting for transfers between devices, on_device(): up_shard = lax.psum_scatter(gu, 'dp', scatter_dimension=0, tiled=True)  46.3 us
    reduce_scatter x1, waiting for transfers between devices, on_device(): down_shard = lax.psum_scatter(gd, 'dp', scatter_dimension=0, tiled=True).T  44.4 us
    pallas_call x1, Pallas kernels, bwd_own(): pl.pallas_call(lambda *r: bwd_own_kernel(*r, blk=blk, **kw), grid_spec=pl...  18.5 us
    all_gather x1, blocking collectives, on_device(): small = lax.all_gather(small, 'tensor', axis=0)  14.9 us
  transfers between devices with their start and end apart: 8, of which 6 were waited for; matrix products, arithmetic and copies ran while one was open for 7% of the time, Pallas kernels for 22%

profile of v1, /device:TPU:0, one launch (start us, length us, event | category | flops | bytes accessed | tf_op | source)
XLA Modules:
  0.0 558.6 jit_solution(15933287930622750805)
XLA Ops:
  7.3 1.9 fusion.2
  9.2 1.6 dynamic-slice_convert_fusion.1
  11.0 1.6 dynamic-slice_convert_fusion
  12.8 14.9 %all-gather = f32[4,1,1152]{2,1,0:T(1,128)S(1)} all-gather(f32[1,1,1152]{2,1,0:T(1,128)S(1)} %fusion.3), channel_id=1, replica_groups=mesh['dp'=8,'tensor'=4] {'tensor'}, dimensions={0}, use_global_device_ids=true | all-gather | bytes 23040 | tf_op jit(solution)/shard_map/all_gather | solution.py:534
  27.7 0.6 slice.67.r_5_
  28.5 0.1 concatenate.39
  28.6 0.6 reshape.124.r_4_
  29.3 0.6 pad_add_fusion.r_1_
  29.9 2.1 fusion.r_3_
  32.0 4.2 pad_maximum_fusion
  36.2 15.0 %attn_fwd.2 = (bf16[4,2048,768]{2,1,0:T(8,128)(2,1)}, bf16[4,2048,256]{2,1,0:T(8,128)(2,1)}) custom-call(s32[1]{0:T(128)} %bitcast.5.r_0_, s32[5]{0:T(128)} %pad_add_fusion.r_1_, bf16[2048,768]{1,0:T(8,128)(2,1)} %get-tuple-element.89.r_2_.r_1_, bf16[1,768,768]{2,1,0:T(8,128)(2,1)} %fusion.r_3_, f32[4,1,768]{2,1,0:T(1,128)} %reshape.124.r_4_), custom_call_target="tpu_custom_call" | custom-call | tf_op jit(solution)/shard_map/attn_fwd/pallas_call | solution.py:117
  51.2 0.5 and_select_fusion.r_0_
  51.7 0.7 maximum_convert_fusion.r_4_
  52.4 43.3 %all-gather.5.cloned.1.call-done = f32[3072,768]{1,0:T(8,128)} async-done(((f32[96,768]{1,0:T(8,128)}), f32[3072,768]{1,0:T(8,128)}) %all-gather.5.cloned.1.call-update) | async-done | bytes 9437200 | tf_op jit(solution)/shard_map/all_gather | solution.py:496
  95.7 39.3 %attn_fwd.3 = (bf16[4,2048,768]{2,1,0:T(8,128)(2,1)}, bf16[4,2048,256]{2,1,0:T(8,128)(2,1)}) custom-call(s32[3]{0:T(128)} %and_select_fusion.r_0_, s32[5]{0:T(128)} %pad_add_fusion.r_1_, bf16[2048,768]{1,0:T(8,128)(2,1)} %get-tuple-element.89.r_2_.r_1_, f32[4,768,768]{2,1,0:T(8,128)} %bitcast.43, ...), custom_call_target="tpu_custom_call", output_to_operand_aliasing={{0}: (5, {}), {1}: (6, {})} | custom-call | tf_op jit(solution)/shard_map/attn_fwd/pallas_call | solution.py:117
  135.1 44.3 %all-gather.7.cloned.1.call-done = f32[3072,768]{1,0:T(8,128)} async-done(((f32[96,768]{1,0:T(8,128)}), f32[3072,768]{1,0:T(8,128)}) %all-gather.7.cloned.1.call-update) | async-done | bytes 9437200 | tf_op jit(solution)/shard_map/all_gather | solution.py:496
  179.3 83.6 %all-gather.9.cloned.1.call-done = f32[3072,768]{1,0:T(8,128)} async-done(((f32[96,768]{1,0:T(8,128)}), f32[3072,768]{1,0:T(8,128)}) %all-gather.9.cloned.1.call-update) | async-done | bytes 9437200 | tf_op jit(solution)/shard_map/all_gather | solution.py:496
  262.9 80.1 %ffn_block.1 = (bf16[2048,768]{1,0:T(8,128)(2,1)}, f32[2048,768]{1,0:T(8,128)}, bf16[4,2048,256]{2,1,0:T(8,128)(2,1)}, f32[768,768]{1,0:T(8,128)}, f32[768,768]{...) custom-call(s32[1]{0:T(128)} %bitcast.5.r_0_, bf16[2048,768]{1,0:T(8,128)(2,1)} %get-tuple-element.89.r_2_.r_1_, ...), custom_call_target="tpu_custom_call" | custom-call | tf_op jit(solution)/shard_map/ffn_block/pallas_call | solution.py:444
  343.0 1.0 reduce_sum.19
  344.0 0.9 copy.53
  345.0 0.5 reduce-scatter.11.cloned.1.call-update
  345.6 18.5 %attn_bwd_own.1 = (bf16[2048,768]{1,0:T(8,128)(2,1)}, f32[768,768]{1,0:T(8,128)}, f32[8,768]{1,0:T(8,128)}) custom-call(s32[1]{0:T(128)} %bitcast.5.r_0_, bf16[2048,768]{1,0:T(8,128)(2,1)} %get-tuple-element.89.r_2_.r_1_, bf16[4,2048,768]{2,1,0:T(8,128)(2,1)} %get-tuple-element.31.r_2_.r_1_, bf16[4,2048,256]{2,1,0:T(8,128)(2,1)} %get-tuple-element.29.r_3_.r_2_, ...), custom_call_target="tpu_custom_call" | custom-call | tf_op jit(solution)/shard_map/attn_bwd_own/pallas_call | solution.py:218
  364.0 2.0 copy.45
  366.1 1.3 slice.70
  367.4 2.8 copy.49
  370.3 0.7 reduce-scatter.15.cloned.1.call-update
  371.0 0.7 reduce-scatter.13.cloned.1.call-update
  371.7 0.6 dynamic-slice
  373.0 0.6 pad_add_fusion.1.r_0_
  373.6 51.0 %attn_bwd_rest.1 = f32[2048,768]{1,0:T(8,128)} custom-call(s32[4]{0:T(128)} %pad_add_fusion.1.r_0_, bf16[4,2048,768]{2,1,0:T(8,128)(2,1)} %get-tuple-element.31.r_2_.r_1_, bf16[4,2048,256]{2,1,0:T(8,128)(2,1)} %get-tuple-element.29.r_3_.r_2_, bf16[4,2048,256]{2,1,0:T(8,128)(2,1)} %get-tuple-element.32.r_4_.r_3_, bf16[2048,768]{1,0:T(8,128)(2,1)} %get-tuple-element.33.r_4_, ...), custom_call_target="tpu_custom_call" | custom-call | tf_op jit(solution)/shard_map/attn_bwd_rest/pallas_call | solution.py:284
  424.6 5.1 slice.69
  429.7 2.8 slice.68
  432.5 1.6 slice.53
  434.1 0.9 slice.52
  435.2 13.4 %all-reduce = f32[2,3,64]{2,1,0:T(4,128)S(1)} all-reduce(f32[2,3,64]{2,1,0:T(4,128)S(1)} %reshape.135), channel_id=3, replica_groups=mesh['dp'=8,'tensor'=4] {'dp'}, use_global_device_ids=true, to_apply=%region_2.3.clone | all-reduce | flops 384 | bytes 3072
  448.6 0.6 copy.47
  449.2 0.9 slice.76
  450.1 1.0 fusion.5
  451.1 0.6 copy.58
  451.8 0.6 copy.59
  452.4 0.6 copy.60
  453.0 0.6 copy.61
  453.6 1.6 copy.48
  455.2 3.9 reduce-scatter.17.cloned.1.call-done
  459.2 1.1 copy.50
  460.2 0.9 copy.46
  461.1 44.4 %reduce-scatter.15.cloned.1.call-done = f32[96,768]{1,0:T(8,128)} async-done(((f32[768,768]{1,0:T(8,128)}), f32[96,768]{1,0:T(8,128)}) %reduce-scatter.15.cloned.1.call-update) | async-done | bytes 294928 | tf_op jit(solution)/shard_map/reduce_scatter | solution.py:561
  505.5 46.3 %reduce-scatter.13.cloned.1.call-done = f32[96,768]{1,0:T(8,128)} async-done(((f32[768,768]{1,0:T(8,128)}), f32[96,768]{1,0:T(8,128)}) %reduce-scatter.13.cloned.1.call-update) | async-done | bytes 294928 | tf_op jit(solution)/shard_map/reduce_scatter | solution.py:560
  (64 shorter events, 1.0 us)
Async XLA Ops:
  7.2 21.3 %copy-start.10 = (f32[64]{0:T(128)S(1)}, f32[64]{0:T(128)}, u32[]{:S(2)}) copy-start(f32[64]{0:T(128)} %constant.48) | copy-start | bytes 772
  7.2 22.7 %copy-start = (bf16[3,768,192]{1,2,0:T(8,128)(2,1)S(1)}, bf16[3,768,192]{1,2,0:T(8,128)(2,1)}, u32[]{:S(2)}) copy-start(bf16[3,768,192]{1,2,0:T(8,128)(2,1)} %param.20) | copy-start | bytes 2654212
  7.2 5.5 copy-start.9
  7.2 5.6 copy-start.8
  7.2 22.1 %copy-start.13 = (s32[2]{0:T(128)S(1)}, s32[2]{0:T(128)}, u32[]{:S(2)}) copy-start(s32[2]{0:T(128)} %param.17) | copy-start | bytes 28
  7.2 22.1 %copy-start.12 = (s32[3]{0:T(128)S(1)}, s32[3]{0:T(128)}, u32[]{:S(2)}) copy-start(s32[3]{0:T(128)} %param.19) | copy-start | bytes 40
  7.2 24.7 %copy-start.2 = (bf16[3,512,768]{2,1,0:T(8,128)(2,1)S(1)}, bf16[3,512,768]{2,1,0:T(8,128)(2,1)}, u32[]{:S(2)}) copy-start(bf16[3,512,768]{2,1,0:T(8,128)(2,1)} %param.18) | copy-start | bytes 7077892
  7.3 88.5 %all-gather.5.cloned.1.call-start = ((), (), s32[]{:S(2)}) async-start(), calls=%async_computation.5 | async-start | bytes 9732096 | tf_op jit(solution)/shard_map/all_gather | solution.py:496
  9.2 170.1 %all-gather.7.cloned.1.call-start = ((), (), s32[]{:S(2)}) async-start(), calls=%async_computation.6 | async-start | bytes 9732096 | tf_op jit(solution)/shard_map/all_gather | solution.py:496
  10.9 252.0 %all-gather.9.cloned.1.call-start = ((), (), s32[]{:S(2)}) async-start(), calls=%async_computation.7 | async-start | bytes 9732096 | tf_op jit(solution)/shard_map/all_gather | solution.py:496
  12.6 436.6 %reduce-scatter.19.cloned.1.call-start = ((), (), s32[]{:S(2)}) async-start(), calls=%async_computation.12 | async-start | bytes 442368
  29.2 2.8 copy-start.3
  36.2 15.5 %copy-start.5 = (bf16[2,768]{1,0:T(2,128)(2,1)S(1)}, bf16[2,768]{1,0:T(2,128)(2,1)}, u32[]{:S(2)}) copy-start(bf16[2,768]{1,0:T(2,128)(2,1)} %param.25) | copy-start | bytes 9220
  36.2 15.5 %copy-start.6 = (bf16[2,768]{1,0:T(2,128)(2,1)S(1)}, bf16[2,768]{1,0:T(2,128)(2,1)}, u32[]{:S(2)}) copy-start(bf16[2,768]{1,0:T(2,128)(2,1)} %param.24) | copy-start | bytes 9220
  36.2 15.5 %copy-start.7 = (bf16[2,768]{1,0:T(2,128)(2,1)S(1)}, bf16[2,768]{1,0:T(2,128)(2,1)}, u32[]{:S(2)}) copy-start(bf16[2,768]{1,0:T(2,128)(2,1)} %param.23) | copy-start | bytes 9220
  344.9 108.7 %reduce-scatter.11.cloned.1.call-start = ((), (), s32[]{:S(2)}) async-start(), calls=%async_computation.8 | async-start | bytes 884736 | tf_op jit(solution)/shard_map/reduce_scatter | solution.py:562
  345.5 113.6 %reduce-scatter.17.cloned.1.call-start = ((), (), s32[]{:S(2)}) async-start(), calls=%async_computation.11 | async-start | bytes 2211840
  370.2 1.5 copy-start.14
  370.2 2.8 copy-start.11
  370.2 135.3 %reduce-scatter.15.cloned.1.call-start = ((), (), s32[]{:S(2)}) async-start(), calls=%async_computation.10 | async-start | bytes 2654208 | tf_op jit(solution)/shard_map/reduce_scatter | solution.py:561
  371.0 180.8 %reduce-scatter.13.cloned.1.call-start = ((), (), s32[]{:S(2)}) async-start(), calls=%async_computation.9 | async-start | bytes 2654208 | tf_op jit(solution)/shard_map/reduce_scatter | solution.py:560
  429.7 2.9 copy-start.1
  432.5 2.5 copy-start.4
Sparse Core Ops, SparseCore 0:
  11.5 84.1 all-gather.4
  99.2 80.0 all-gather.6
  182.8 80.0 all-gather.8
  345.1 32.4 reduce-scatter.18
  380.5 34.9 reduce-scatter.10
  418.8 40.3 reduce-scatter.16
  463.1 42.3 reduce-scatter.14
  509.4 42.3 reduce-scatter.12
